TPU v7x, 256 devices: a whole 4x4x8 slice. The times are simulated.
256 devices in a mesh: lon: 32 (over y, z), lat: 8 (over x, core).
Axes of the slice: x: 4, y: 4, z: 8, core: 2. Of those that a mesh axis runs over, the one named last changes fastest.
Arguments:
- height: float32 [1024, 512, 1024], P(None, 'lon', 'lat'), may hold values from -1 to 1
- land_sea: int32 [512, 1024], P('lon', 'lat'), may hold values 0 or 1
- patterns: bfloat16 [512, 2, 512, 1024], P(None, None, 'lon', 'lat'), may hold values from -0.01171875 to 0.01171875
Outputs:
- covariance: float32 [32, 512, 512], P('lon', 'lat')
All inputs are finite; a program needn't handle non-finite values. No bound on the sum of `land_sea` on one device may be relied on, other than what follows from the above.
Results may differ from a plain program's by a relative error of at most 0.0003.
The roundings to bfloat16 on the way count: a program that leaves them out, or rounds other values in their place, can miss the bound.
Values sent between devices are 32-bit elements; how exact they have to be, the bound alone decides.
A program may use at most 128 MiB of HBM per device.

v0:
```python
import math
import jax
import jax.numpy as jnp
from jax import lax
from jax.sharding import PartitionSpec as P

LAG_DEV = 1
GRAVITY = 9.81
ROTATION = 7.2921e-05
EARTH_RADIUS = 6371000.0
LAT_SOUTH = 20.0
LAT_SPAN = 45.0
LON_STEP = 1.0 / 12.0


def padded_2(shard, sides, width):
    for axis, dim in sides:
        devices, length = (lax.axis_size(axis), shard.shape[dim])
        up = [(i, (i + 1) % devices) for i in range(devices - 1)]
        down = [(j, i) for i, j in up]
        last = lax.slice_in_dim(shard, length - width, length, axis=dim)
        initial = lax.slice_in_dim(shard, 0, width, axis=dim)
        before = lax.ppermute(last, axis, up)
        after = lax.ppermute(initial, axis, down)
        shard = jnp.concatenate([before, shard, after], axis=dim)
    return shard


def stencil_coefs(rows_index, total_rows):
    degrees = LAT_SOUTH + LAT_SPAN * (rows_index.astype(jnp.float32) + 0.5) / total_rows
    radians = degrees * (math.pi / 180.0)
    coriolis = 2.0 * ROTATION * jnp.sin(radians)
    north_step = EARTH_RADIUS * (LAT_SPAN / total_rows) * (math.pi / 180.0)
    east_step = EARTH_RADIUS * jnp.cos(radians) * (LON_STEP * math.pi / 180.0)
    return (-GRAVITY / (coriolis * 2.0 * north_step), GRAVITY / (coriolis * 2.0 * east_step))


def velocities(padded, coef_east, coef_north, ocean):
    lat_diff = padded[:, 1:-1, 2:] - padded[:, 1:-1, :-2]
    lon_diff = padded[:, 2:, 1:-1] - padded[:, :-2, 1:-1]
    return (coef_east * lat_diff * ocean, coef_north * lon_diff * ocean)


def on_device(height, land_sea, patterns):
    days, lon_cells, lat_cells = height.shape
    lat_devices = lax.axis_size("lat")
    lon_devices = lax.axis_size("lon")
    total_rows = lat_cells * lat_devices
    lat_place = lax.axis_index("lat")
    lon_place = lax.axis_index("lon")
    rows_index = lat_place * lat_cells + jnp.arange(lat_cells, dtype=jnp.int32)
    coef_east, coef_north = stencil_coefs(rows_index, total_rows)
    ocean = land_sea.astype(jnp.float32)
    padded = padded_2(height, (("lon", 1), ("lat", 2)), 1)
    east_vel, north_vel = velocities(padded, coef_east, coef_north, ocean)
    local_energy = jnp.sum(east_vel * east_vel + north_vel * north_vel)
    stacked = (
        jnp.stack([east_vel, north_vel], axis=1)
        .astype(jnp.bfloat16)
        .reshape(days, 2 * lon_cells * lat_cells)
    )
    mode_count = patterns.shape[0]
    owned = mode_count // lat_devices
    flat_patterns = patterns.reshape(mode_count, 2 * lon_cells * lat_cells)
    energy = lax.psum(local_energy, ("lon", "lat"))
    totals = lax.psum(
        lax.dot_general(
            flat_patterns, stacked, (((1,), (1,)), ((), ())), preferred_element_type=jnp.float32
        ),
        ("lon", "lat"),
    )
    cell_total = 2.0 * days * lon_cells * lon_devices * total_rows
    centered = totals - jnp.mean(totals, axis=1, keepdims=True)
    normed = centered / jnp.sqrt(energy / cell_total + 1e-06)
    my_rows = lax.dynamic_slice_in_dim(normed, lat_place * owned, owned, 0)
    padded_rows = jnp.concatenate([my_rows, jnp.zeros_like(my_rows)], axis=1)
    lag = lon_place * LAG_DEV + 0
    shifted = lax.dynamic_slice_in_dim(padded_rows, lag, days, 1)
    product = lax.dot_general(
        shifted,
        normed,
        (((1,), (1,)), ((), ())),
        precision=lax.Precision.HIGHEST,
        preferred_element_type=jnp.float32,
    )
    results = [product / (days - lag).astype(jnp.float32)]
    return jnp.stack(results, axis=0)


def solution(mesh):
    placed = (P(None, "lon", "lat"), P("lon", "lat"), P(None, None, "lon", "lat"))
    return jax.shard_map(
        on_device, mesh=mesh, in_specs=placed, out_specs=P("lon", "lat", None), check_vma=False
    )
```

profile of v0, /device:TPU:2, one launch (start us, length us, event | category | flops | bytes accessed | tf_op | source)
XLA Modules:
  0.0 381.3 jit_solution(7635947852473987990)
XLA Ops:
  6.5 0.0 copy-start.2
  6.5 0.0 all-reduce.3.cloned.1.call-start
  6.5 6.1 %copy.10 = f32[1024,16,128]{2,0,1:T(8,128)S(1)} copy(f32[1024,16,128]{2,1,0:T(8,128)} %param.3) | data formatting | bytes 16777216 | tf_op args[0]
  12.6 0.0 copy-start.1
  12.6 3.3 copy-done.1
  15.9 0.1 fusion.23
  16.0 3.9 %collective-permute-start = (f32[1024,1,128]{2,0,1:T(8,128)S(1)}, f32[1024,1,128]{2,0,1:T(8,128)S(1)}, u32[]{:S(2)}, u32[]{:S(2)}) collective-permute-start(f32[1024,1,128]{2,0,1:T(8,128)S(1)} %get-tuple-element.11), channel_id=1, source_target_pairs={{0,8},{8,16},{16,24},{24,32},{32,40},{40,48},{48,56},{56,64},{64,7... | collective-permute-start | bytes 1572872 | tf_op jit(solution)/shard_map/ppermute | solution.py:23
  19.9 1.3 collective-permute-start.1
  21.2 0.0 copy-done.2
  21.2 9.8 %collective-permute-done = f32[1024,1,128]{2,0,1:T(8,128)S(1)} collective-permute-done((f32[1024,1,128]{2,0,1:T(8,128)S(1)}, f32[1024,1,128]{2,0,1:T(8,128)S(1)}, u32[]{:S(2)}, u32[]{:S(2)}) %collective-permute-start) | collective-permute-done | bytes 524320 | tf_op jit(solution)/shard_map/ppermute | solution.py:23
  31.0 5.8 %constant_dynamic-update-slice_fusion.1 = f32[1024,18,128]{2,0,1:T(8,128)S(1)} fusion(f32[1024,18,128]{2,0,1:T(8,128)S(1)} %constant_dynamic-update-slice_fusion.2, f32[1024,16,128]{2,1,0:T(8,128)} %param.3), kind=kLoop, calls=%fused_computation.24 | loop fusion | bytes 16777216
  36.8 0.0 collective-permute-done.1
  36.9 0.0 copy-start
  36.9 8.4 %fusion.22 = (f32[1024,18,1]{2,0,1:T(8,128)}, f32[1024,18,1]{2,0,1:T(8,128)}) fusion(f32[1024,18,128]{2,0,1:T(8,128)S(1)} %constant_dynamic-update-slice_fusion), kind=kLoop, calls=%fused_computation.35 | loop fusion | bytes 294912 | tf_op jit(solution)/shard_map/slice | solution.py:22
  45.3 0.9 copy-done
  46.2 5.6 %copy.13 = f32[1024,18,1]{0,2,1:T(1,128)S(1)} copy(f32[1024,18,1]{2,0,1:T(8,128)} %get-tuple-element.8) | data formatting | bytes 147456 | tf_op jit(solution)/shard_map/slice | solution.py:22
  51.8 1.9 collective-permute-start.2
  53.7 5.6 %copy.15 = f32[1024,18,1]{0,2,1:T(1,128)S(1)} copy(f32[1024,18,1]{2,0,1:T(8,128)} %get-tuple-element.9) | data formatting | bytes 147456 | tf_op jit(solution)/shard_map/slice | solution.py:21
  59.3 2.6 collective-permute-start.3
  61.9 0.1 multiply_divide_fusion
  62.0 0.0 collective-permute-done.2
  62.0 5.1 %copy.14 = f32[1024,18,1]{2,0,1:T(8,128)} copy(f32[1024,18,1]{0,2,1:T(1,128)S(1)} %collective-permute-done.2) | data formatting | bytes 147456 | tf_op jit(solution)/shard_map/ppermute | solution.py:24
  67.1 0.0 collective-permute-done.3
  67.1 5.2 %copy.16 = f32[1024,18,1]{2,0,1:T(8,128)} copy(f32[1024,18,1]{0,2,1:T(1,128)S(1)} %collective-permute-done.3) | data formatting | bytes 147456 | tf_op jit(solution)/shard_map/ppermute | solution.py:23
  72.2 18.3 %add_reduce_fusion = (f32[]{:T(128)}, bf16[1024,16,128]{2,0,1:T(8,128)(2,1)S(1)}, bf16[1024,1,16,128]{3,0,2,1:T(8,128)(2,1)S(1)}) fusion(f32[16,128]{1,0:T(8,128)S(1)} %convert_element_type.18, f32[1024,16,128]{2,0,1:T(8,128)} %copy-done.1, f32[1024,1,128]{2,0,1:T(8,128)S(1)} %collective-permute-done, f32[1024,1,128]{2,0,1:T(8,128)S(1)} %collective-permute-done.1, ...), kind=kLoop, calls=%fused_computation.14 | loop fusion | flops 33554432 | bytes 27419652 | tf_op jit(solution)/shard_map/reduce_sum | solution.py:56
  90.5 8.1 %fusion.11 = f32[512,1024]{0,1:T(8,128)} fusion(bf16[512,2,16,128]{3,2,1,0:T(8,128)(2,1)} %param.5, bf16[1024,1,16,128]{3,0,2,1:T(8,128)(2,1)S(1)} %get-tuple-element.7, bf16[1024,1,16,128]{3,0,2,1:T(8,128)(2,1)S(1)} %bitcast.14), kind=kOutput, calls=%fused_computation.19 | convolution fusion | flops 4299161600 | bytes 14680064 | tf_op jit(solution)/shard_map/dot_general | solution.py:67
  98.6 0.0 all-reduce.3.cloned.1.call-update
  98.7 80.3 %psum.15 = f32[]{:T(128)} all-reduce(f32[]{:T(128)} %get-tuple-element.5), channel_id=1, replica_groups=mesh['lon'=32,'lat'=8] {'lon','lat'}, use_global_device_ids=true, to_apply=%region_3.0 | all-reduce | flops 1 | bytes 8 | tf_op jit(solution)/shard_map/psum | solution.py:65
  179.7 188.9 %all-reduce.3.cloned.1.call-done = f32[512,1024]{0,1:T(8,128)} async-done(((f32[512,1024]{0,1:T(8,128)}), f32[512,1024]{0,1:T(8,128)}) %all-reduce.3.cloned.1.call-update) | async-done | bytes 2097168 | tf_op jit(solution)/shard_map/psum | solution.py:66
  368.6 1.8 reduce_sum.18
  370.4 1.9 subtract_divide_fusion
  372.2 0.2 constant_dynamic-slice_fusion
  372.4 2.0 fusion.16
  (4 shorter events, 0.1 us)
Async XLA Ops:
  6.5 14.6 %copy-start.2 = (s32[16,128]{1,0:T(8,128)S(1)}, s32[16,128]{1,0:T(8,128)}, u32[]{:S(2)}) copy-start(s32[16,128]{1,0:T(8,128)} %param.4) | copy-start | bytes 24580
  6.5 362.0 %all-reduce.3.cloned.1.call-start = ((), (), s32[]{:S(2)}) async-start(), calls=%async_computation | async-start | bytes 4194304 | tf_op jit(solution)/shard_map/psum | solution.py:66
  12.6 3.3 copy-start.1
  16.0 15.0 %collective-permute-start = (f32[1024,1,128]{2,0,1:T(8,128)S(1)}, f32[1024,1,128]{2,0,1:T(8,128)S(1)}, u32[]{:S(2)}, u32[]{:S(2)}) collective-permute-start(f32[1024,1,128]{2,0,1:T(8,128)S(1)} %get-tuple-element.11), channel_id=1, source_target_pairs={{0,8},{8,16},{16,24},{24,32},{32,40},{40,48},{48,56},{56,64},{64,7... | collective-permute-start | bytes 1572872 | tf_op jit(solution)/shard_map/ppermute | solution.py:23
  19.9 17.0 %collective-permute-start.1 = (f32[1024,1,128]{2,0,1:T(8,128)S(1)}, f32[1024,1,128]{2,0,1:T(8,128)S(1)}, u32[]{:S(2)}, u32[]{:S(2)}) collective-permute-start(f32[1024,1,128]{2,0,1:T(8,128)S(1)} %get-tuple-element.10), channel_id=1, source_target_pairs={{8,0},{16,8},{24,16},{32,24},{40,32},{48,40},{56,48},{64,56},{72,6... | collective-permute-start | bytes 1572872 | tf_op jit(solution)/shard_map/ppermute | solution.py:24
  36.9 9.3 %copy-start = (f32[1024,18,128]{2,0,1:T(8,128)}, f32[1024,18,128]{2,0,1:T(8,128)S(1)}, u32[]{:S(2)}) copy-start(f32[1024,18,128]{2,0,1:T(8,128)S(1)} %constant_dynamic-update-slice_fusion) | copy-start | bytes 28311556
  51.8 10.2 %collective-permute-start.2 = (f32[1024,18,1]{0,2,1:T(1,128)S(1)}, f32[1024,18,1]{0,2,1:T(1,128)S(1)}, u32[]{:S(2)}, u32[]{:S(2)}) collective-permute-start(f32[1024,18,1]{0,2,1:T(1,128)S(1)} %copy.13), channel_id=1, source_target_pairs={{1,0},{2,1},{3,2},{4,3},{5,4},{6,5},{7,6},{9,8},{10,9},{11,10},{12... | collective-permute-start | bytes 221192 | tf_op jit(solution)/shard_map/ppermute | solution.py:24
  59.3 7.8 %collective-permute-start.3 = (f32[1024,18,1]{0,2,1:T(1,128)S(1)}, f32[1024,18,1]{0,2,1:T(1,128)S(1)}, u32[]{:S(2)}, u32[]{:S(2)}) collective-permute-start(f32[1024,18,1]{0,2,1:T(1,128)S(1)} %copy.15), channel_id=1, source_target_pairs={{0,1},{1,2},{2,3},{3,4},{4,5},{5,6},{6,7},{8,9},{9,10},{10,11},{11... | collective-permute-start | bytes 221192 | tf_op jit(solution)/shard_map/ppermute | solution.py:23
Sparse Core Ops, SparseCore 0:
  98.8 269.7 all-reduce.2
where the time goes:
time: 382 us; the launch traced here: 381 us
  waiting for transfers between devices  199 us (52%)
  blocking collectives  80.3 us (21%)
  local copies, waits for them, and re-layouts  46.3 us (12%)
  other arithmetic  22 us (6%)
  between operations  14.2 us (4%)
  matrix products  10.1 us (3%)
  starting transfers between devices  9.66 us (3%)
    psum x1, waiting for transfers between devices, on_device(): lax.psum(lax.dot_general(flat_patterns, stacked, (((1,), (1,)), ((), ()))...  189 us
    psum x1, blocking collectives, on_device(): energy = lax.psum(local_energy, ('lon', 'lat'))  80.3 us
    reduce_sum x1, other arithmetic, on_device(): local_energy = jnp.sum(east_vel * east_vel + north_vel * north_vel)  18.3 us
    unnamed x9, local copies, waits for them, and re-layouts  16.1 us
    slice x3, local copies, waits for them, and re-layouts, padded_2(): initial = lax.slice_in_dim(shard, 0, width, axis=dim)  14.1 us
    ppermute x2, waiting for transfers between devices, padded_2(): before = lax.ppermute(last, axis, up)  9.8 us
    dot_general x1, matrix products, on_device(): lax.dot_general(flat_patterns, stacked, (((1,), (1,)), ((), ())), preferr...  8.1 us
  transfers between devices with their start and end apart: 5, of which 2 were waited for; matrix products, arithmetic and copies ran while one was open for 4% of the time, Pallas kernels for 0%

commit v1 on v0

--- a/solution.py
+++ b/solution.py
@@ -64,10 +64,13 @@
     flat_patterns = patterns.reshape(mode_count, 2 * lon_cells * lat_cells)
     energy = lax.psum(local_energy, ("lon", "lat"))
     totals = lax.psum(
-        lax.dot_general(
-            flat_patterns, stacked, (((1,), (1,)), ((), ())), preferred_element_type=jnp.float32
+        lax.psum(
+            lax.dot_general(
+                flat_patterns, stacked, (((1,), (1,)), ((), ())), preferred_element_type=jnp.float32
+            ),
+            "lon",
         ),
-        ("lon", "lat"),
+        "lat",
     )
     cell_total = 2.0 * days * lon_cells * lon_devices * total_rows
     centered = totals - jnp.mean(totals, axis=1, keepdims=True)

time: 382 us -> 348 us (0.911)
  waiting for transfers between devices: 199 us -> 169 us
  blocking collectives: 80.3 us -> 72.8 us
    psum x1, waiting for transfers between devices: 189 us -> 160 us  [on_device(): lax.psum(lax.dot_general(flat_patterns, stacked, (((1,), (1,)), ((), ()))...]
    psum x1, blocking collectives: 80.3 us -> 72.8 us  [on_device(): energy = lax.psum(local_energy, ('lon', 'lat'))]
  transfers between devices with their start and end apart: 5 -> 6, of which waited for: 2 -> 2; matrix products, arithmetic and copies ran while one was open for 4% -> 5% of each run, Pallas kernels for 0% -> 0%
where the time goes in v1:
time: 348 us; the launch traced here: 345 us
  waiting for transfers between devices  169 us (49%)
  blocking collectives  72.8 us (21%)
  local copies, waits for them, and re-layouts  46.3 us (13%)
  other arithmetic  22 us (6%)
  between operations  14.2 us (4%)
  matrix products  10.1 us (3%)
  starting transfers between devices  9.7 us (3%)
    psum x1, waiting for transfers between devices, on_device(): lax.psum(lax.dot_general(flat_patterns, stacked, (((1,), (1,)), ((), ()))...  160 us
    psum x1, blocking collectives, on_device(): energy = lax.psum(local_energy, ('lon', 'lat'))  72.8 us
    reduce_sum x1, other arithmetic, on_device(): local_energy = jnp.sum(east_vel * east_vel + north_vel * north_vel)  18.3 us
    unnamed x9, local copies, waits for them, and re-layouts  16.1 us
    slice x3, local copies, waits for them, and re-layouts, padded_2(): initial = lax.slice_in_dim(shard, 0, width, axis=dim)  14.1 us
    ppermute x2, waiting for transfers between devices, padded_2(): before = lax.ppermute(last, axis, up)  9.8 us
    dot_general x1, matrix products, on_device(): lax.dot_general(flat_patterns, stacked, (((1,), (1,)), ((), ())), preferr...  8.1 us
  transfers between devices with their start and end apart: 6, of which 2 were waited for; matrix products, arithmetic and copies ran while one was open for 5% of the time, Pallas kernels for 0%

profile of v1, /device:TPU:2, one launch (start us, length us, event | category | flops | bytes accessed | tf_op | source)
XLA Modules:
  0.0 344.6 jit_solution(16123550296219267547)
XLA Ops:
  6.5 0.0 copy-start.2
  6.5 0.0 all-reduce.4.cloned.1.call-start
  6.5 6.1 %copy.10 = f32[1024,16,128]{2,0,1:T(8,128)S(1)} copy(f32[1024,16,128]{2,1,0:T(8,128)} %param.3) | data formatting | bytes 16777216 | tf_op args[0]
  12.6 0.0 copy-start.1
  12.6 3.3 copy-done.1
  15.9 0.1 fusion.23
  16.0 3.9 %collective-permute-start = (f32[1024,1,128]{2,0,1:T(8,128)S(1)}, f32[1024,1,128]{2,0,1:T(8,128)S(1)}, u32[]{:S(2)}, u32[]{:S(2)}) collective-permute-start(f32[1024,1,128]{2,0,1:T(8,128)S(1)} %get-tuple-element.11), channel_id=1, source_target_pairs={{0,8},{8,16},{16,24},{24,32},{32,40},{40,48},{48,56},{56,64},{64,7... | collective-permute-start | bytes 1572872 | tf_op jit(solution)/shard_map/ppermute | solution.py:23
  19.9 1.3 collective-permute-start.1
  21.2 0.0 copy-done.2
  21.2 9.8 %collective-permute-done = f32[1024,1,128]{2,0,1:T(8,128)S(1)} collective-permute-done((f32[1024,1,128]{2,0,1:T(8,128)S(1)}, f32[1024,1,128]{2,0,1:T(8,128)S(1)}, u32[]{:S(2)}, u32[]{:S(2)}) %collective-permute-start) | collective-permute-done | bytes 524320 | tf_op jit(solution)/shard_map/ppermute | solution.py:23
  31.0 5.8 %constant_dynamic-update-slice_fusion.1 = f32[1024,18,128]{2,0,1:T(8,128)S(1)} fusion(f32[1024,18,128]{2,0,1:T(8,128)S(1)} %constant_dynamic-update-slice_fusion.2, f32[1024,16,128]{2,1,0:T(8,128)} %param.3), kind=kLoop, calls=%fused_computation.24 | loop fusion | bytes 16777216
  36.8 0.0 collective-permute-done.1
  36.9 0.0 copy-start
  36.9 8.4 %fusion.22 = (f32[1024,18,1]{2,0,1:T(8,128)}, f32[1024,18,1]{2,0,1:T(8,128)}) fusion(f32[1024,18,128]{2,0,1:T(8,128)S(1)} %constant_dynamic-update-slice_fusion), kind=kLoop, calls=%fused_computation.35 | loop fusion | bytes 294912 | tf_op jit(solution)/shard_map/slice | solution.py:22
  45.3 0.9 copy-done
  46.2 5.6 %copy.13 = f32[1024,18,1]{0,2,1:T(1,128)S(1)} copy(f32[1024,18,1]{2,0,1:T(8,128)} %get-tuple-element.8) | data formatting | bytes 147456 | tf_op jit(solution)/shard_map/slice | solution.py:22
  51.8 1.9 collective-permute-start.2
  53.7 5.6 %copy.15 = f32[1024,18,1]{0,2,1:T(1,128)S(1)} copy(f32[1024,18,1]{2,0,1:T(8,128)} %get-tuple-element.9) | data formatting | bytes 147456 | tf_op jit(solution)/shard_map/slice | solution.py:21
  59.3 2.6 collective-permute-start.3
  61.9 0.1 multiply_divide_fusion
  62.0 0.0 collective-permute-done.2
  62.0 5.1 %copy.14 = f32[1024,18,1]{2,0,1:T(8,128)} copy(f32[1024,18,1]{0,2,1:T(1,128)S(1)} %collective-permute-done.2) | data formatting | bytes 147456 | tf_op jit(solution)/shard_map/ppermute | solution.py:24
  67.1 0.0 collective-permute-done.3
  67.1 5.2 %copy.16 = f32[1024,18,1]{2,0,1:T(8,128)} copy(f32[1024,18,1]{0,2,1:T(1,128)S(1)} %collective-permute-done.3) | data formatting | bytes 147456 | tf_op jit(solution)/shard_map/ppermute | solution.py:23
  72.2 18.3 %add_reduce_fusion = (f32[]{:T(128)}, bf16[1024,16,128]{2,0,1:T(8,128)(2,1)S(1)}, bf16[1024,1,16,128]{3,0,2,1:T(8,128)(2,1)S(1)}) fusion(f32[16,128]{1,0:T(8,128)S(1)} %convert_element_type.18, f32[1024,16,128]{2,0,1:T(8,128)} %copy-done.1, f32[1024,1,128]{2,0,1:T(8,128)S(1)} %collective-permute-done, f32[1024,1,128]{2,0,1:T(8,128)S(1)} %collective-permute-done.1, ...), kind=kLoop, calls=%fused_computation.14 | loop fusion | flops 33554432 | bytes 27419652 | tf_op jit(solution)/shard_map/reduce_sum | solution.py:56
  90.5 8.1 %fusion.11 = f32[512,1024]{0,1:T(8,128)} fusion(bf16[512,2,16,128]{3,2,1,0:T(8,128)(2,1)} %param.5, bf16[1024,1,16,128]{3,0,2,1:T(8,128)(2,1)S(1)} %get-tuple-element.7, bf16[1024,1,16,128]{3,0,2,1:T(8,128)(2,1)S(1)} %bitcast.14), kind=kOutput, calls=%fused_computation.19 | convolution fusion | flops 4299161600 | bytes 14680064 | tf_op jit(solution)/shard_map/dot_general | solution.py:68
  98.6 0.0 all-reduce.4.cloned.1.call-update
  98.7 0.0 all-reduce.6.cloned.1.call-start
  98.7 159.6 %all-reduce.4.cloned.1.call-done = f32[512,1024]{0,1:T(8,128)} async-done(((f32[512,1024]{0,1:T(8,128)}), f32[512,1024]{0,1:T(8,128)}) %all-reduce.4.cloned.1.call-update) | async-done | bytes 2097168 | tf_op jit(solution)/shard_map/psum | solution.py:67
  258.3 0.0 all-reduce.6.cloned.1.call-update
  258.3 72.8 %psum.23 = f32[]{:T(128)} all-reduce(f32[]{:T(128)} %get-tuple-element.5), channel_id=1, replica_groups=mesh['lon'=32,'lat'=8] {'lon','lat'}, use_global_device_ids=true, to_apply=%region_4.0 | all-reduce | flops 1 | bytes 8 | tf_op jit(solution)/shard_map/psum | solution.py:65
  331.8 0.0 all-reduce.6.cloned.1.call-done
  331.8 1.8 reduce_sum.18
  333.6 1.9 subtract_divide_fusion
  335.5 0.2 constant_dynamic-slice_fusion
  335.7 2.0 fusion.16
  (4 shorter events, 0.1 us)
Async XLA Ops:
  6.5 14.6 %copy-start.2 = (s32[16,128]{1,0:T(8,128)S(1)}, s32[16,128]{1,0:T(8,128)}, u32[]{:S(2)}) copy-start(s32[16,128]{1,0:T(8,128)} %param.4) | copy-start | bytes 24580
  6.5 251.8 %all-reduce.4.cloned.1.call-start = ((), (), s32[]{:S(2)}) async-start(), calls=%async_computation | async-start | bytes 4194304 | tf_op jit(solution)/shard_map/psum | solution.py:67
  12.6 3.3 copy-start.1
  16.0 15.0 %collective-permute-start = (f32[1024,1,128]{2,0,1:T(8,128)S(1)}, f32[1024,1,128]{2,0,1:T(8,128)S(1)}, u32[]{:S(2)}, u32[]{:S(2)}) collective-permute-start(f32[1024,1,128]{2,0,1:T(8,128)S(1)} %get-tuple-element.11), channel_id=1, source_target_pairs={{0,8},{8,16},{16,24},{24,32},{32,40},{40,48},{48,56},{56,64},{64,7... | collective-permute-start | bytes 1572872 | tf_op jit(solution)/shard_map/ppermute | solution.py:23
  19.9 17.0 %collective-permute-start.1 = (f32[1024,1,128]{2,0,1:T(8,128)S(1)}, f32[1024,1,128]{2,0,1:T(8,128)S(1)}, u32[]{:S(2)}, u32[]{:S(2)}) collective-permute-start(f32[1024,1,128]{2,0,1:T(8,128)S(1)} %get-tuple-element.10), channel_id=1, source_target_pairs={{8,0},{16,8},{24,16},{32,24},{40,32},{48,40},{56,48},{64,56},{72,6... | collective-permute-start | bytes 1572872 | tf_op jit(solution)/shard_map/ppermute | solution.py:24
  36.9 9.3 %copy-start = (f32[1024,18,128]{2,0,1:T(8,128)}, f32[1024,18,128]{2,0,1:T(8,128)S(1)}, u32[]{:S(2)}) copy-start(f32[1024,18,128]{2,0,1:T(8,128)S(1)} %constant_dynamic-update-slice_fusion) | copy-start | bytes 28311556
  51.8 10.2 %collective-permute-start.2 = (f32[1024,18,1]{0,2,1:T(1,128)S(1)}, f32[1024,18,1]{0,2,1:T(1,128)S(1)}, u32[]{:S(2)}, u32[]{:S(2)}) collective-permute-start(f32[1024,18,1]{0,2,1:T(1,128)S(1)} %copy.13), channel_id=1, source_target_pairs={{1,0},{2,1},{3,2},{4,3},{5,4},{6,5},{7,6},{9,8},{10,9},{11,10},{12... | collective-permute-start | bytes 221192 | tf_op jit(solution)/shard_map/ppermute | solution.py:24
  59.3 7.8 %collective-permute-start.3 = (f32[1024,18,1]{0,2,1:T(1,128)S(1)}, f32[1024,18,1]{0,2,1:T(1,128)S(1)}, u32[]{:S(2)}, u32[]{:S(2)}) collective-permute-start(f32[1024,18,1]{0,2,1:T(1,128)S(1)} %copy.15), channel_id=1, source_target_pairs={{0,1},{1,2},{2,3},{3,4},{4,5},{5,6},{6,7},{8,9},{9,10},{10,11},{11... | collective-permute-start | bytes 221192 | tf_op jit(solution)/shard_map/ppermute | solution.py:23
  98.7 233.1 %all-reduce.6.cloned.1.call-start = ((), (), s32[]{:S(2)}) async-start(), calls=%async_computation.1 | async-start | bytes 4194304 | tf_op jit(solution)/shard_map/psum | solution.py:66
Sparse Core Ops, SparseCore 0:
  98.8 159.4 all-reduce.3
  260.7 65.8 all-reduce.5
